TPU v7x, 32 devices: a whole 2x2x4 slice. The times are simulated.
32 devices in a mesh: tok: 8 (over z, x), tp: 4 (over y, core).
Axes of the slice: x: 2, y: 2, z: 4, core: 2. Of those that a mesh axis runs over, the one named last changes fastest.
Arguments:
- resid: bfloat16 [1024, 8192], P('tok', 'tp'), may hold values from -7 to 7
- norm_gain: float32 [8192], P('tp'), may hold values from 0.5 to 1.5
- head_in: bfloat16 [8192, 2048], P('tp'), may hold values from -0.088388348 to 0.088388348
- head_bias: float32 [2048], replicated, may hold values from -3 to 3
- head_out: float32 [16, 128], replicated, may hold values from -0.26516504 to 0.26516504
- targets: float32 [1024, 16], P('tok'), may hold values from -12 to 12
- label_mask: int32 [1024, 16], P('tok'), may hold values 0 or 1
- obj_weight: int32 [16], replicated, may hold values from 1 to 16
Outputs:
- resid_grad: bfloat16 [1024, 8192], P('tok', 'tp')
- gain_grad: float32 [8192], P('tp')
- head_in_grad: float32 [8192, 2048], P('tp', 'tok')
- head_bias_grad: float32 [2048], replicated
All inputs are finite; a program needn't handle non-finite values. No bound on the sum of `label_mask` on one device may be relied on, other than what follows from the above.
Results may differ from a plain program's by a relative error of at most 0.0078.
Values may be sent and summed in bfloat16 or wider, within the bound.
No kernel may reach another device: no remote copies, remote signals or barrier semaphores. Data moves between devices by JAX's collectives and lax.ppermute only.
A program may use at most 128 MiB of HBM per device.

v0:
```python
import jax
import jax.numpy as jnp
from jax import lax
from jax.sharding import PartitionSpec as P

D = 8192
norm_eps = 1e-05
grad_eps = 1e-06
denominator = 8.0


def head_gradient(preact, head_out, targets, label_mask):
    count = preact.shape[0]
    objectives, hidden = head_out.shape
    cube = preact.reshape(count, objectives, hidden)
    squash = jax.nn.sigmoid(cube)
    scores = jnp.sum(cube * squash * head_out[None], axis=2)
    errors = label_mask.astype(jnp.float32) * (scores - targets)
    slopes = squash * (1.0 + cube * (1.0 - squash))
    row_grad = (errors[:, :, None] * head_out[None] * slopes).astype(jnp.bfloat16)
    return row_grad.reshape(count, objectives * hidden)


def per_device(resid, norm_gain, head_in, head_bias, head_out, targets, label_mask, obj_weight):
    tok_rows = resid.shape[0]
    objectives, hidden = head_out.shape
    total_tokens = tok_rows * lax.axis_size("tok")
    floated = resid.astype(jnp.float32)
    row_sums = lax.psum(jnp.sum(floated * floated, axis=1), "tp")
    inverse = lax.rsqrt(row_sums[:, None] / D + norm_eps)
    unit = floated * inverse
    normed = (unit * norm_gain[None, :]).astype(jnp.bfloat16)
    partial_value = jnp.dot(normed, head_in, preferred_element_type=jnp.float32)
    quarter = lax.psum_scatter(partial_value, "tp", scatter_dimension=0, tiled=True)
    share = quarter.shape[0]
    offset = lax.axis_index("tp") * share
    part_targets = lax.dynamic_slice_in_dim(targets, offset, share, 0)
    part_mask = lax.dynamic_slice_in_dim(label_mask, offset, share, 0)
    part_grad = head_gradient(quarter + head_bias[None, :], head_out, part_targets, part_mask)
    row_grad = lax.all_gather(part_grad, "tp", axis=0, tiled=True)
    grad_float = row_grad.astype(jnp.float32)

    def objective_square(which):
        grad_slice = lax.dynamic_slice_in_dim(row_grad, which * hidden, hidden, 1)
        weight_slice = lax.dynamic_slice_in_dim(head_in, which * hidden, hidden, 1)
        feature_grad = lax.dot_general(
            grad_slice, weight_slice, (((1,), (1,)), ((), ())), preferred_element_type=jnp.float32
        )
        return jnp.sum(feature_grad * feature_grad)

    local_squares = lax.map(objective_square, jnp.arange(objectives))
    squares = lax.psum(local_squares, ("tok", "tp"))
    obj_rms = jnp.sqrt(squares / (total_tokens * D) + grad_eps)
    balance = obj_weight.astype(jnp.float32) / denominator / obj_rms
    balance_cols = jnp.repeat(balance, hidden)
    pre_grad = (grad_float * balance_cols[None, :]).astype(jnp.bfloat16)
    norm_grad = lax.dot_general(
        pre_grad, head_in, (((1,), (1,)), ((), ())), preferred_element_type=jnp.float32
    )
    gain_sum, bias_sum = lax.psum(
        (jnp.sum(norm_grad * unit, axis=0), jnp.sum(grad_float, axis=0)), "tok"
    )
    gain_grad = gain_sum / total_tokens
    head_bias_grad = bias_sum * balance_cols / total_tokens
    projection = lax.psum(jnp.sum(unit * norm_gain[None, :] * norm_grad, axis=1), "tp")
    resid_grad = (
        inverse * (norm_gain[None, :] * norm_grad - unit * (projection[:, None] / D))
    ).astype(jnp.bfloat16)
    weight_term = lax.dot_general(
        normed, row_grad, (((0,), (0,)), ((), ())), preferred_element_type=jnp.float32
    )
    summed_block = lax.psum_scatter(weight_term, "tok", scatter_dimension=1, tiled=True)
    columns = summed_block.shape[1]
    col_scale = lax.dynamic_slice_in_dim(balance_cols, lax.axis_index("tok") * columns, columns, 0)
    head_in_grad = summed_block * col_scale[None, :] / total_tokens
    return (resid_grad, gain_grad, head_in_grad, head_bias_grad)


def solution(mesh):
    return jax.shard_map(
        per_device,
        mesh=mesh,
        in_specs=(
            P("tok", "tp"),
            P("tp"),
            P("tp", None),
            P(),
            P(),
            P("tok", None),
            P("tok", None),
            P(),
        ),
        out_specs=(P("tok", "tp"), P("tp"), P("tp", "tok"), P()),
        check_vma=False,
    )
```

profile of v0, /device:TPU:0, one launch (start us, length us, event | category | flops | bytes accessed | tf_op | source)
XLA Modules:
  0.0 359.1 jit_solution(12255660014555638462)
XLA Ops:
  8.5 8.4 %psum.35 = f32[128]{0:T(128)S(1)} all-reduce(f32[128]{0:T(128)S(1)} %fusion.14), channel_id=1, replica_groups=mesh['tok'=8,'tp'=4] {'tp'}, use_global_device_ids=true, to_apply=%region_1.0 | all-reduce | flops 128 | bytes 1024 | tf_op jit(solution)/shard_map/psum | solution.py:29
  16.9 5.9 %fusion.26 = f32[128,2048]{1,0:T(8,128)} fusion(bf16[2048,2048]{1,0:T(8,128)(2,1)} %param.12, bf16[128,2048]{1,0:T(8,128)(2,1)} %param.10, f32[2048]{0:T(1024)} %param.11, f32[128]{0:T(128)S(1)} %add_rsqrt_fusion), kind=kOutput, calls=%fused_computation.35 | convolution fusion | flops 1074790400 | bytes 9970176 | tf_op jit(solution)/shard_map/dot_general | solution.py:33
  23.2 24.9 %reduce-scatter.3.cloned.1.call-done = f32[32,2048]{1,0:T(8,128)} async-done(((f32[128,2048]{1,0:T(8,128)}), f32[32,2048]{1,0:T(8,128)}) %reduce-scatter.3.cloned.1.call-update) | async-done | bytes 262160 | tf_op jit(solution)/shard_map/reduce_scatter | solution.py:34
  50.6 6.6 %all_gather.3 = bf16[128,2048]{1,0:T(8,128)(2,1)S(1)} all-gather(bf16[32,2048]{1,0:T(8,128)(2,1)S(1)} %fusion.20), channel_id=1, replica_groups=mesh['tok'=8,'tp'=4] {'tp'}, dimensions={0}, use_global_device_ids=true | all-gather | bytes 655360 | tf_op jit(solution)/shard_map/all_gather | solution.py:40
  57.3 8.2 %fusion.24 = f32[2048,2048]{1,0:T(8,128)} fusion(bf16[128,2048]{1,0:T(8,128)(2,1)S(1)} %all_gather.3, bf16[128,2048]{1,0:T(8,128)(2,1)S(1)} %copy-done.1, f32[2048]{0:T(1024)S(1)} %copy-done.2, f32[128]{0:T(128)S(1)} %add_rsqrt_fusion), kind=kOutput, calls=%fused_computation.34 | convolution fusion | flops 1074790400 | bytes 17834496 | tf_op jit(solution)/shard_map/dot_general | solution.py:69
  65.5 65.5 %while.10 = (s32[]{:T(128)}, f32[16]{0:T(128)S(1)}, s32[16]{0:T(128)S(1)}, bf16[128,2048]{1,0:T(8,128)(2,1)S(1)}, bf16[2048,2048]{1,0:T(8,128)(2,1)}, /*index=5*/s32[]{:T(128)}, s32[1]{0:T(128)}, s32[]{:T(128)}, s32[]{:T(128)}) while((s32[]{:T(128)}, f32[16]{0:T(128)S(1)}, s32[16]{0:T(128)S(1)}, bf16[128,2048]{1,0:T(8,128)(2,1)S(1)}, ...), condition=%wide.region_6.7_spmd, body=%wide.region_4.6_spmd.sunk | while | flops 67633160 | bytes 558255 | solution.py:51
  70.8 2.1 fusion.36
  74.9 2.1 fusion.36
  79.0 2.1 fusion.36
  83.1 2.1 fusion.36
  91.3 2.1 fusion.36
  95.4 2.1 fusion.36
  99.5 2.1 fusion.36
  103.6 2.1 fusion.36
  107.7 2.1 fusion.36
  111.8 2.1 fusion.36
  120.0 2.1 fusion.36
  128.1 2.1 fusion.36
  131.0 43.7 %psum.36 = f32[16]{0:T(128)S(1)} all-reduce(f32[16]{0:T(128)S(1)} %get-tuple-element.31), channel_id=1, replica_groups=mesh['tok'=8,'tp'=4] {'tok','tp'}, use_global_device_ids=true, to_apply=%region_7.8 | all-reduce | flops 16 | bytes 128 | tf_op jit(solution)/shard_map/psum | solution.py:52
  174.9 6.6 %fusion.13 = (f32[2048]{0:T(1024)S(1)}, f32[128]{0:T(128)S(1)}, f32[128,2048]{1,0:T(8,128)S(1)}) fusion(bf16[128,2048]{1,0:T(8,128)(2,1)S(1)} %copy-done.1, f32[128]{0:T(128)S(1)} %add_rsqrt_fusion, f32[2048]{0:T(1024)S(1)} %copy-done.2, bf16[2048,2048]{1,0:T(8,128)(2,1)} %get-tuple-element.111, bf16[128,2048]{1,0:T(8,128)(2,1)S(1)} %get-tuple-element.112, ...), kind=kOutput, calls=%fused_computation.19 | convolution fusion | flops 1076361088 | bytes 10511360 | tf_op jit(solution)/shard_map/dot_general | solution.py:57
  181.5 6.1 %psum.37 = f32[128]{0:T(128)S(1)} all-reduce(f32[128]{0:T(128)S(1)} %get-tuple-element.33), channel_id=1, replica_groups=mesh['tok'=8,'tp'=4] {'tp'}, use_global_device_ids=true, to_apply=%region_9.10 | all-reduce | flops 128 | bytes 1024 | tf_op jit(solution)/shard_map/psum | solution.py:65
  187.7 37.6 %all-reduce = (f32[2048]{0:T(1024)S(1)}, f32[2048]{0:T(1024)S(1)}) all-reduce(f32[2048]{0:T(1024)S(1)} %get-tuple-element.32, f32[2048]{0:T(1024)S(1)} %convert_reduce_fusion), channel_id=1, replica_groups=mesh['tok'=8,'tp'=4] {'tok'}, use_global_device_ids=true, to_apply=%region_11.12 | all-reduce | flops 4096 | bytes 32768 | tf_op jit(solution)/shard_map/psum | solution.py:60
  227.1 122.1 %reduce-scatter.5.cloned.1.call-done = f32[2048,256]{1,0:T(8,128)} async-done(((f32[2048,2048]{1,0:T(8,128)}), f32[2048,256]{1,0:T(8,128)}) %reduce-scatter.5.cloned.1.call-update) | async-done | bytes 2097168 | tf_op jit(solution)/shard_map/reduce_scatter | solution.py:72
  349.2 3.0 multiply_multiply_fusion
  (76 shorter events, 36.0 us)
Async XLA Ops:
  7.2 15.7 %copy-start = (s32[128,16]{0,1:T(8,128)S(1)}, s32[128,16]{0,1:T(8,128)}, u32[]{:S(2)}) copy-start(s32[128,16]{0,1:T(8,128)} %param.16) | copy-start | bytes 24580
  7.2 40.9 %reduce-scatter.3.cloned.1.call-start = ((), (), s32[]{:S(2)}) async-start(), calls=%async_computation.2 | async-start | bytes 1310720 | tf_op jit(solution)/shard_map/reduce_scatter | solution.py:34
  16.9 6.2 %copy-start.5 = (f32[128,16]{0,1:T(8,128)S(1)}, f32[128,16]{0,1:T(8,128)}, u32[]{:S(2)}) copy-start(f32[128,16]{0,1:T(8,128)} %param.15) | copy-start | bytes 24580
  16.9 31.3 %copy-start.3 = (f32[2048]{0:T(1024)S(1)}, f32[2048]{0:T(1024)}, u32[]{:S(2)}) copy-start(f32[2048]{0:T(1024)} %param.13) | copy-start | bytes 24580
  16.9 32.4 %copy-start.4 = (f32[16,128]{1,0:T(8,128)S(1)}, f32[16,128]{1,0:T(8,128)}, u32[]{:S(2)}) copy-start(f32[16,128]{1,0:T(8,128)} %param.14) | copy-start | bytes 24580
  16.9 40.4 %copy-start.1 = (bf16[128,2048]{1,0:T(8,128)(2,1)S(1)}, bf16[128,2048]{1,0:T(8,128)(2,1)}, u32[]{:S(2)}) copy-start(bf16[128,2048]{1,0:T(8,128)(2,1)} %param.10) | copy-start | bytes 1572868
  16.9 40.4 %copy-start.2 = (f32[2048]{0:T(1024)S(1)}, f32[2048]{0:T(1024)}, u32[]{:S(2)}) copy-start(f32[2048]{0:T(1024)} %param.11) | copy-start | bytes 24580
  22.8 326.3 %reduce-scatter.5.cloned.1.call-start = ((), (), s32[]{:S(2)}) async-start(), calls=%async_computation.3 | async-start | bytes 18874368 | tf_op jit(solution)/shard_map/reduce_scatter | solution.py:72
  65.4 109.3 %copy-start.6 = (s32[16]{0:T(128)S(1)}, s32[16]{0:T(128)}, u32[]{:S(2)}) copy-start(s32[16]{0:T(128)} %param.17) | copy-start | bytes 196
Sparse Core Ops, SparseCore 0:
  22.9 25.1 reduce-scatter.2
  65.6 283.5 reduce-scatter.4
where the time goes:
time: 361 us; the launch traced here: 359 us
  waiting for transfers between devices  147 us (41%)
  blocking collectives  102 us (28%)
  matrix products  54.3 us (15%)
  local copies, waits for them, and re-layouts  22.1 us (6%)
  between operations  14.2 us (4%)
  loops' own time  10.5 us (3%)
  other arithmetic  8.51 us (2%)
    reduce_scatter x1, waiting for transfers between devices, per_device(): lax.psum_scatter(weight_term, 'tok', scatter_dimension=1, tiled=True)  122 us
    psum x1, blocking collectives, per_device(): squares = lax.psum(local_squares, ('tok', 'tp'))  43.7 us
    psum x1, blocking collectives, per_device(): lax.psum((jnp.sum(norm_grad * unit, axis=0), jnp.sum(grad_float, axis=0))...  37.6 us
    dot_general x16, matrix products, objective_square(): lax.dot_general(grad_slice, weight_slice, (((1,), (1,)), ((), ())), prefe...  33.5 us
    reduce_scatter x1, waiting for transfers between devices, per_device(): lax.psum_scatter(partial_value, 'tp', scatter_dimension=0, tiled=True)  24.9 us
    dynamic_update_slice x16, local copies, waits for them, and re-layouts, per_device(): local_squares = lax.map(objective_square, jnp.arange(objectives))  12.1 us
    another operation x1, loops' own time, per_device(): local_squares = lax.map(objective_square, jnp.arange(objectives))  10.5 us
    dynamic_slice x16, local copies, waits for them, and re-layouts, per_device(): local_squares = lax.map(objective_square, jnp.arange(objectives))  9.33 us
  transfers between devices with their start and end apart: 2, of which 2 were waited for; matrix products, arithmetic and copies ran while one was open for 18% of the time, Pallas kernels for 0%

commit v1 on v0

--- a/solution.py
+++ b/solution.py
@@ -49,7 +49,7 @@
         return jnp.sum(feature_grad * feature_grad)
 
     local_squares = lax.map(objective_square, jnp.arange(objectives))
-    squares = lax.psum(local_squares, ("tok", "tp"))
+    squares = lax.psum(lax.psum(local_squares, "tp"), "tok")
     obj_rms = jnp.sqrt(squares / (total_tokens * D) + grad_eps)
     balance = obj_weight.astype(jnp.float32) / denominator / obj_rms
     balance_cols = jnp.repeat(balance, hidden)

time: 361 us -> 359 us (level)
  blocking collectives: 102 us -> 86.1 us
  waiting for transfers between devices: 147 us -> 162 us
    reduce_scatter x1, waiting for transfers between devices: 122 us -> 137 us  [per_device(): lax.psum_scatter(weight_term, 'tok', scatter_dimension=1, tiled=True)]
    psum x1 -> x2, blocking collectives: 43.7 us -> 29.3 us  [per_device(): squares = lax.psum(lax.psum(local_squares, 'tp'), 'tok')]
where the time goes in v1:
time: 359 us; the launch traced here: 358 us
  waiting for transfers between devices  162 us (45%)
  blocking collectives  86.1 us (24%)
  matrix products  54.1 us (15%)
  local copies, waits for them, and re-layouts  22.1 us (6%)
  between operations  14.2 us (4%)
  loops' own time  10.5 us (3%)
  other arithmetic  8.51 us (2%)
    reduce_scatter x1, waiting for transfers between devices, per_device(): lax.psum_scatter(weight_term, 'tok', scatter_dimension=1, tiled=True)  137 us
    psum x1, blocking collectives, per_device(): lax.psum((jnp.sum(norm_grad * unit, axis=0), jnp.sum(grad_float, axis=0))...  35.7 us
    dot_general x16, matrix products, objective_square(): lax.dot_general(grad_slice, weight_slice, (((1,), (1,)), ((), ())), prefe...  33.5 us
    psum x2, blocking collectives, per_device(): squares = lax.psum(lax.psum(local_squares, 'tp'), 'tok')  29.3 us
    reduce_scatter x1, waiting for transfers between devices, per_device(): lax.psum_scatter(partial_value, 'tp', scatter_dimension=0, tiled=True)  24.9 us
    dynamic_update_slice x16, local copies, waits for them, and re-layouts, per_device(): local_squares = lax.map(objective_square, jnp.arange(objectives))  12.1 us
    another operation x1, loops' own time, per_device(): local_squares = lax.map(objective_square, jnp.arange(objectives))  10.5 us
    dynamic_slice x16, local copies, waits for them, and re-layouts, per_device(): local_squares = lax.map(objective_square, jnp.arange(objectives))  9.33 us
  transfers between devices with their start and end apart: 2, of which 2 were waited for; matrix products, arithmetic and copies ran while one was open for 18% of the time, Pallas kernels for 0%

profile of v1, /device:TPU:0, one launch (start us, length us, event | category | flops | bytes accessed | tf_op | source)
XLA Modules:
  0.0 357.6 jit_solution(12243835203068716780)
XLA Ops:
  8.5 8.4 %psum.42 = f32[128]{0:T(128)S(1)} all-reduce(f32[128]{0:T(128)S(1)} %fusion.14), channel_id=1, replica_groups=mesh['tok'=8,'tp'=4] {'tp'}, use_global_device_ids=true, to_apply=%region_1.0 | all-reduce | flops 128 | bytes 1024 | tf_op jit(solution)/shard_map/psum | solution.py:29
  16.9 5.9 %fusion.26 = f32[128,2048]{1,0:T(8,128)} fusion(bf16[2048,2048]{1,0:T(8,128)(2,1)} %param.12, bf16[128,2048]{1,0:T(8,128)(2,1)} %param.10, f32[2048]{0:T(1024)} %param.11, f32[128]{0:T(128)S(1)} %add_rsqrt_fusion), kind=kOutput, calls=%fused_computation.35 | convolution fusion | flops 1074790400 | bytes 9970176 | tf_op jit(solution)/shard_map/dot_general | solution.py:33
  23.2 24.9 %reduce-scatter.3.cloned.1.call-done = f32[32,2048]{1,0:T(8,128)} async-done(((f32[128,2048]{1,0:T(8,128)}), f32[32,2048]{1,0:T(8,128)}) %reduce-scatter.3.cloned.1.call-update) | async-done | bytes 262160 | tf_op jit(solution)/shard_map/reduce_scatter | solution.py:34
  50.6 6.6 %all_gather.3 = bf16[128,2048]{1,0:T(8,128)(2,1)S(1)} all-gather(bf16[32,2048]{1,0:T(8,128)(2,1)S(1)} %fusion.20), channel_id=1, replica_groups=mesh['tok'=8,'tp'=4] {'tp'}, dimensions={0}, use_global_device_ids=true | all-gather | bytes 655360 | tf_op jit(solution)/shard_map/all_gather | solution.py:40
  57.3 8.2 %fusion.24 = f32[2048,2048]{1,0:T(8,128)} fusion(bf16[128,2048]{1,0:T(8,128)(2,1)S(1)} %all_gather.3, bf16[128,2048]{1,0:T(8,128)(2,1)S(1)} %copy-done.1, f32[2048]{0:T(1024)S(1)} %copy-done.2, f32[128]{0:T(128)S(1)} %add_rsqrt_fusion), kind=kOutput, calls=%fused_computation.34 | convolution fusion | flops 1074790400 | bytes 17834496 | tf_op jit(solution)/shard_map/dot_general | solution.py:69
  65.5 65.5 %while.10 = (s32[]{:T(128)}, f32[16]{0:T(128)S(1)}, s32[16]{0:T(128)S(1)}, bf16[128,2048]{1,0:T(8,128)(2,1)S(1)}, bf16[2048,2048]{1,0:T(8,128)(2,1)}, /*index=5*/s32[]{:T(128)}, s32[1]{0:T(128)}, s32[]{:T(128)}, s32[]{:T(128)}) while((s32[]{:T(128)}, f32[16]{0:T(128)S(1)}, s32[16]{0:T(128)S(1)}, bf16[128,2048]{1,0:T(8,128)(2,1)S(1)}, ...), condition=%wide.region_6.7_spmd, body=%wide.region_4.6_spmd.sunk | while | flops 67633160 | bytes 558255 | solution.py:51
  70.8 2.1 fusion.36
  74.9 2.1 fusion.36
  79.0 2.1 fusion.36
  83.1 2.1 fusion.36
  91.3 2.1 fusion.36
  99.5 2.1 fusion.36
  103.6 2.1 fusion.36
  107.7 2.1 fusion.36
  111.8 2.1 fusion.36
  120.0 2.1 fusion.36
  128.1 2.1 fusion.36
  131.0 7.0 %psum.43 = f32[16]{0:T(128)S(1)} all-reduce(f32[16]{0:T(128)S(1)} %get-tuple-element.31), channel_id=1, replica_groups=mesh['tok'=8,'tp'=4] {'tp'}, use_global_device_ids=true, to_apply=%region_7.8 | all-reduce | flops 16 | bytes 128 | tf_op jit(solution)/shard_map/psum | solution.py:52
  138.0 22.3 %psum.44 = f32[16]{0:T(128)S(1)} all-reduce(f32[16]{0:T(128)S(1)} %psum.43), channel_id=1, replica_groups=mesh['tok'=8,'tp'=4] {'tok'}, use_global_device_ids=true, to_apply=%region_8.9 | all-reduce | flops 16 | bytes 128 | tf_op jit(solution)/shard_map/psum | solution.py:52
  160.5 6.5 %fusion.13 = (f32[2048]{0:T(1024)S(1)}, f32[128]{0:T(128)S(1)}, f32[128,2048]{1,0:T(8,128)S(1)}) fusion(bf16[128,2048]{1,0:T(8,128)(2,1)S(1)} %copy-done.1, f32[128]{0:T(128)S(1)} %add_rsqrt_fusion, f32[2048]{0:T(1024)S(1)} %copy-done.2, bf16[2048,2048]{1,0:T(8,128)(2,1)} %get-tuple-element.111, bf16[128,2048]{1,0:T(8,128)(2,1)S(1)} %get-tuple-element.112, ...), kind=kOutput, calls=%fused_computation.19 | convolution fusion | flops 1076361088 | bytes 10511360 | tf_op jit(solution)/shard_map/dot_general | solution.py:57
  167.0 6.1 %psum.45 = f32[128]{0:T(128)S(1)} all-reduce(f32[128]{0:T(128)S(1)} %get-tuple-element.33), channel_id=1, replica_groups=mesh['tok'=8,'tp'=4] {'tp'}, use_global_device_ids=true, to_apply=%region_10.11 | all-reduce | flops 128 | bytes 1024 | tf_op jit(solution)/shard_map/psum | solution.py:65
  173.2 35.7 %all-reduce = (f32[2048]{0:T(1024)S(1)}, f32[2048]{0:T(1024)S(1)}) all-reduce(f32[2048]{0:T(1024)S(1)} %get-tuple-element.32, f32[2048]{0:T(1024)S(1)} %convert_reduce_fusion), channel_id=1, replica_groups=mesh['tok'=8,'tp'=4] {'tok'}, use_global_device_ids=true, to_apply=%region_12.13 | all-reduce | flops 4096 | bytes 32768 | tf_op jit(solution)/shard_map/psum | solution.py:60
  210.7 137.0 %reduce-scatter.5.cloned.1.call-done = f32[2048,256]{1,0:T(8,128)} async-done(((f32[2048,2048]{1,0:T(8,128)}), f32[2048,256]{1,0:T(8,128)}) %reduce-scatter.5.cloned.1.call-update) | async-done | bytes 2097168 | tf_op jit(solution)/shard_map/reduce_scatter | solution.py:72
  347.7 3.0 multiply_multiply_fusion
  (77 shorter events, 38.1 us)
Async XLA Ops:
  7.2 15.7 %copy-start = (s32[128,16]{0,1:T(8,128)S(1)}, s32[128,16]{0,1:T(8,128)}, u32[]{:S(2)}) copy-start(s32[128,16]{0,1:T(8,128)} %param.16) | copy-start | bytes 24580
  7.2 40.9 %reduce-scatter.3.cloned.1.call-start = ((), (), s32[]{:S(2)}) async-start(), calls=%async_computation.2 | async-start | bytes 1310720 | tf_op jit(solution)/shard_map/reduce_scatter | solution.py:34
  16.9 6.2 %copy-start.5 = (f32[128,16]{0,1:T(8,128)S(1)}, f32[128,16]{0,1:T(8,128)}, u32[]{:S(2)}) copy-start(f32[128,16]{0,1:T(8,128)} %param.15) | copy-start | bytes 24580
  16.9 31.3 %copy-start.3 = (f32[2048]{0:T(1024)S(1)}, f32[2048]{0:T(1024)}, u32[]{:S(2)}) copy-start(f32[2048]{0:T(1024)} %param.13) | copy-start | bytes 24580
  16.9 32.4 %copy-start.4 = (f32[16,128]{1,0:T(8,128)S(1)}, f32[16,128]{1,0:T(8,128)}, u32[]{:S(2)}) copy-start(f32[16,128]{1,0:T(8,128)} %param.14) | copy-start | bytes 24580
  16.9 40.4 %copy-start.1 = (bf16[128,2048]{1,0:T(8,128)(2,1)S(1)}, bf16[128,2048]{1,0:T(8,128)(2,1)}, u32[]{:S(2)}) copy-start(bf16[128,2048]{1,0:T(8,128)(2,1)} %param.10) | copy-start | bytes 1572868
  16.9 40.4 %copy-start.2 = (f32[2048]{0:T(1024)S(1)}, f32[2048]{0:T(1024)}, u32[]{:S(2)}) copy-start(f32[2048]{0:T(1024)} %param.11) | copy-start | bytes 24580
  22.8 324.9 %reduce-scatter.5.cloned.1.call-start = ((), (), s32[]{:S(2)}) async-start(), calls=%async_computation.3 | async-start | bytes 18874368 | tf_op jit(solution)/shard_map/reduce_scatter | solution.py:72
  65.4 94.9 %copy-start.6 = (s32[16]{0:T(128)S(1)}, s32[16]{0:T(128)}, u32[]{:S(2)}) copy-start(s32[16]{0:T(128)} %param.17) | copy-start | bytes 196
Sparse Core Ops, SparseCore 0:
  22.9 25.1 reduce-scatter.2
  65.6 282.0 reduce-scatter.4
